TPU v7x, 32 devices: a whole 2x2x4 slice. The times are simulated.
32 devices in a mesh: seq: 8 (over z, y), tp: 4 (over x, core).
Axes of the slice: x: 2, y: 2, z: 4, core: 2. Of those that a mesh axis runs over, the one named last changes fastest.
Arguments:
- inputs: bfloat16 [16, 1024, 768], P(None, 'seq'), may hold values from -6 to 6
- lengths: int32 [16], replicated, may hold values from 256 to 1024, as said below
- first_gain: float32 [768], replicated, may hold values from 0.5 to 1.5
- query_weight: bfloat16 [768, 768], P(None, 'tp'), may hold values from -0.21875 to 0.21875
- key_weight: bfloat16 [768, 768], P(None, 'tp'), may hold values from -0.21875 to 0.21875
- value_weight: bfloat16 [768, 768], P(None, 'tp'), may hold values from -0.21875 to 0.21875
- shift_taps: float32 [4, 768], P(None, 'tp'), may hold values from -3 to 3
- state_coef: float32 [768, 64], P('tp'), may hold values from -0.1875 to 0.1875
- state_rate: float32 [768, 64], P('tp'), may hold values from 0.00048828125 to 0.2
- skip_gain: float32 [768], P('tp'), may hold values from -3 to 3
- project_weight: bfloat16 [768, 768], P('tp'), may hold values from -0.21875 to 0.21875
- second_gain: float32 [768], replicated, may hold values from 0.5 to 1.5
- up_weight: bfloat16 [768, 3072], P(None, 'tp'), may hold values from -0.21875 to 0.21875
- down_weight: bfloat16 [3072, 768], P('tp'), may hold values from -0.109375 to 0.109375
- cotangent: bfloat16 [16, 1024, 768], P(None, 'seq'), may hold values from -6 to 6
Outputs:
- block_out: float32 [16, 1024, 768], P(None, 'seq')
- grad_inputs: float32 [16, 1024, 768], P(None, 'seq')
- grad_first: float32 [768], replicated
- grad_query: float32 [768, 768], P(None, 'tp')
- grad_key: float32 [768, 768], P(None, 'tp')
- grad_value: float32 [768, 768], P(None, 'tp')
- grad_taps: float32 [4, 768], P(None, 'tp')
- grad_coef: float32 [768, 64], P('tp')
- grad_rate: float32 [768, 64], P('tp')
- grad_skip: float32 [768], P('tp')
- grad_project: float32 [768, 768], P('tp')
- grad_second: float32 [768], replicated
- grad_up: float32 [768, 3072], P(None, 'tp')
- grad_down: float32 [3072, 768], P('tp')
Inputs may be any that keep to these rules, and one draw needn't show every extreme that they name: `lengths`: one of the 16 sequences, which one drawn from the seed, has exactly 1024 tokens; positions from a sequence's length on are padding.
All inputs are finite; a program needn't handle non-finite values.
Results may differ from a plain program's by a relative error of at most 0.0075.
Values sent between devices are 32-bit elements; how exact they have to be, the bound alone decides.
No kernel may reach another device: no remote copies, remote signals or barrier semaphores. Data moves between devices by JAX's collectives and lax.ppermute only.
A program may use at most 192 MiB of HBM per device.

v0:
```python
import jax
import jax.numpy as jnp
from jax import lax
from jax.sharding import PartitionSpec as P

exact_mode = lax.Precision.HIGHEST


def passed_along(x, axis, by):
    count = lax.axis_size(axis)
    pairs = [(i, i + by) for i in range(count) if 0 <= i + by < count]
    return lax.ppermute(x, axis, pairs)


def layer_norm(rows, gain):
    center = rows - jnp.mean(rows, axis=-1, keepdims=True)
    spread = jnp.mean(center * center, axis=-1, keepdims=True)
    return center * lax.rsqrt(spread + 1e-05) * gain


def kernel_values(coef, rate, freq, parity, total, length):
    half = jnp.pi * freq / total
    below = jnp.sin(half)
    square = (below * below)[:, None, None]
    whole = jnp.sin(2.0 * half)[:, None, None]
    decay = jnp.exp(-rate)
    gap = -jnp.expm1(-rate)
    ending = jnp.exp(-rate * length)
    numer = 1.0 - parity[:, None, None] * ending
    denom = gap * gap + 4.0 * decay * square
    real_term = numer * (gap + 2.0 * decay * square) / denom
    imag_term = -numer * decay * whole / denom
    return (jnp.sum(coef * real_term, axis=-1), jnp.sum(coef * imag_term, axis=-1))


def angles(left, right, modulus):
    return 2.0 * jnp.pi / modulus * (left[:, None] * right[None, :] % modulus).astype(jnp.float32)


def project(left, right):
    return jnp.einsum("btd,de->bte", left, right, preferred_element_type=jnp.float32)


def to_bins(signal, num_dev, place):
    num_seqs, block_len, channels = signal.shape
    per_dev = block_len // num_dev
    span_len = 2 * num_dev
    total = span_len * block_len
    parted = lax.all_to_all(
        signal.reshape(num_seqs, 1, block_len, channels),
        "seq",
        split_axis=2,
        concat_axis=1,
        tiled=True,
    )
    outer = angles(jnp.arange(num_dev), jnp.arange(span_len), span_len)
    first_re = jnp.einsum("bpmc,pq->bqmc", parted, jnp.cos(outer), precision=exact_mode)
    first_im = -jnp.einsum("bpmc,pq->bqmc", parted, jnp.sin(outer), precision=exact_mode)
    twist = angles(jnp.arange(span_len), place * per_dev + jnp.arange(per_dev), total)
    twist_cos = jnp.cos(twist)[None, :, :, None]
    twist_sin = jnp.sin(twist)[None, :, :, None]
    turned_re = first_re * twist_cos + first_im * twist_sin
    turned_im = first_im * twist_cos - first_re * twist_sin
    joined = lax.all_to_all(
        jnp.stack([turned_re, turned_im]), "seq", split_axis=2, concat_axis=3, tiled=True
    )
    wave = angles(jnp.arange(block_len), jnp.arange(block_len), block_len)
    wave_cos = jnp.cos(wave)
    wave_sin = jnp.sin(wave)
    spec_re = jnp.einsum("bqmc,mj->bqjc", joined[0], wave_cos, precision=exact_mode) + jnp.einsum(
        "bqmc,mj->bqjc", joined[1], wave_sin, precision=exact_mode
    )
    spec_im = jnp.einsum("bqmc,mj->bqjc", joined[1], wave_cos, precision=exact_mode) - jnp.einsum(
        "bqmc,mj->bqjc", joined[0], wave_sin, precision=exact_mode
    )
    return (spec_re, spec_im)


def from_bins(spec_re, spec_im, num_dev, place):
    num_seqs, bin_rows, block_len, channels = spec_re.shape
    span_len = 2 * num_dev
    total = span_len * block_len
    wave = angles(jnp.arange(block_len), jnp.arange(block_len), block_len)
    wave_cos = jnp.cos(wave)
    wave_sin = jnp.sin(wave)
    back_re = jnp.einsum("bqjc,jm->bqmc", spec_re, wave_cos, precision=exact_mode) - jnp.einsum(
        "bqjc,jm->bqmc", spec_im, wave_sin, precision=exact_mode
    )
    back_im = jnp.einsum("bqjc,jm->bqmc", spec_re, wave_sin, precision=exact_mode) + jnp.einsum(
        "bqjc,jm->bqmc", spec_im, wave_cos, precision=exact_mode
    )
    twist = angles(place * bin_rows + jnp.arange(bin_rows), jnp.arange(block_len), total)
    twist_cos = jnp.cos(twist)[None, :, :, None]
    twist_sin = jnp.sin(twist)[None, :, :, None]
    turned_re = back_re * twist_cos - back_im * twist_sin
    turned_im = back_re * twist_sin + back_im * twist_cos
    parted = lax.all_to_all(
        jnp.stack([turned_re, turned_im]), "seq", split_axis=3, concat_axis=2, tiled=True
    )
    outer = angles(jnp.arange(span_len), jnp.arange(num_dev), span_len)
    times_re = (
        jnp.einsum("bqmc,qp->bpmc", parted[0], jnp.cos(outer), precision=exact_mode)
        - jnp.einsum("bqmc,qp->bpmc", parted[1], jnp.sin(outer), precision=exact_mode)
    ) / total
    joined = lax.all_to_all(times_re, "seq", split_axis=1, concat_axis=2, tiled=True)
    return joined.reshape(num_seqs, block_len, channels)


def local(
    inputs,
    lengths,
    first_gain,
    query_weight,
    key_weight,
    value_weight,
    shift_taps,
    state_coef,
    state_rate,
    skip_gain,
    project_weight,
    second_gain,
    up_weight,
    down_weight,
    cotangent,
):
    num_dev = lax.axis_size("seq")
    place = lax.axis_index("seq")
    num_seqs, block_len, width_all = inputs.shape
    tap_count = shift_taps.shape[0]
    seq_len = num_dev * block_len
    total = 2 * seq_len
    source = inputs.astype(jnp.float32)
    positions = place * block_len + jnp.arange(block_len)
    validity = (positions[None, :] < lengths[:, None]).astype(jnp.float32)[:, :, None]
    normed = layer_norm(source, first_gain).astype(jnp.bfloat16)
    queries = project(normed, query_weight)
    key_rows = project(normed, key_weight)
    values = project(normed, value_weight)
    tail = key_rows[:, block_len - (tap_count - 1) :, :]
    before = passed_along(tail, "seq", 1)
    extended = jnp.concatenate([before, key_rows], axis=1)
    shifted = jnp.zeros_like(key_rows)
    for offset in range(tap_count):
        shifted = (
            shifted
            + shift_taps[offset]
            * extended[:, tap_count - 1 - offset : tap_count - 1 - offset + block_len, :]
        )
    mixed_in = shifted * values
    channels = state_coef.shape[0]
    bin_index = place * 2 + jnp.arange(2)
    freq_int = (bin_index[:, None] + 2 * num_dev * jnp.arange(block_len)[None, :]).reshape(-1)
    freq = freq_int.astype(jnp.float32)
    parity = (1 - 2 * (freq_int % 2)).astype(jnp.float32)

    def kernel_part(coef, rate):
        part_re, part_im = kernel_values(coef, rate, freq, parity, total, seq_len)
        return (part_re.reshape(2, block_len, channels), part_im.reshape(2, block_len, channels))

    (kernel_re, kernel_im), kernel_pull = jax.vjp(kernel_part, state_coef, state_rate)
    spec_re, spec_im = to_bins(mixed_in, num_dev, place)
    conv = from_bins(
        spec_re * kernel_re - spec_im * kernel_im,
        spec_re * kernel_im + spec_im * kernel_re,
        num_dev,
        place,
    )
    state_out = conv + skip_gain * mixed_in
    gated_out = (queries * state_out).astype(jnp.bfloat16)
    mixer = lax.psum(project(gated_out, project_weight), "tp")
    residual = source + mixer
    second = layer_norm(residual, second_gain).astype(jnp.bfloat16)
    up_act = project(second, up_weight)
    hidden = jax.nn.gelu(up_act).astype(jnp.bfloat16)
    lowered = lax.psum(project(hidden, down_weight), "tp")
    block_out = validity * (residual + lowered)
    d_mlp = validity * cotangent.astype(jnp.float32)
    d_mlp_low = d_mlp.astype(jnp.bfloat16)
    grad_down = jnp.einsum("btf,btd->fd", hidden, d_mlp_low, preferred_element_type=jnp.float32)
    d_hidden = jnp.einsum("btd,fd->btf", d_mlp_low, down_weight, preferred_element_type=jnp.float32)
    gelu_value, gelu_pull = jax.vjp(jax.nn.gelu, up_act)
    d_up = gelu_pull(d_hidden)[0].astype(jnp.bfloat16)
    grad_up = jnp.einsum("btd,btf->df", second, d_up, preferred_element_type=jnp.float32)
    d_second = lax.psum(
        jnp.einsum("btf,df->btd", d_up, up_weight, preferred_element_type=jnp.float32), "tp"
    )
    norm_value, second_pull = jax.vjp(layer_norm, residual, second_gain)
    d_resid_norm, grad_second = second_pull(d_second)
    d_residual = d_mlp + d_resid_norm
    d_resid_low = d_residual.astype(jnp.bfloat16)
    grad_project = jnp.einsum(
        "btc,btd->cd", gated_out, d_resid_low, preferred_element_type=jnp.float32
    )
    d_gated = jnp.einsum(
        "btd,cd->btc", d_resid_low, project_weight, preferred_element_type=jnp.float32
    )
    d_queries = (d_gated * state_out).astype(jnp.bfloat16)
    d_state = d_gated * queries
    back_re, back_im = to_bins(d_state, num_dev, place)
    fore_re, fore_im = to_bins(lax.optimization_barrier(mixed_in), num_dev, place)
    grad_kernel_re = jnp.sum(back_re * fore_re + back_im * fore_im, axis=0) / total
    grad_kernel_im = jnp.sum(back_im * fore_re - back_re * fore_im, axis=0) / total
    grad_coef, grad_rate = kernel_pull((grad_kernel_re, grad_kernel_im))
    corr = from_bins(
        back_re * kernel_re + back_im * kernel_im,
        back_im * kernel_re - back_re * kernel_im,
        num_dev,
        place,
    )
    d_mixed = corr + skip_gain * d_state
    grad_skip = jnp.sum(d_state * mixed_in, axis=(0, 1))
    d_values = (d_mixed * shifted).astype(jnp.bfloat16)
    d_shifted = d_mixed * values
    d_extended = jnp.zeros_like(extended)
    tap_sums = []
    for offset in range(tap_count):
        d_extended = d_extended + jnp.pad(
            shift_taps[offset] * d_shifted, ((0, 0), (tap_count - 1 - offset, offset), (0, 0))
        )
        tap_sums.append(
            jnp.sum(
                d_shifted
                * extended[:, tap_count - 1 - offset : tap_count - 1 - offset + block_len, :],
                axis=(0, 1),
            )
        )
    grad_taps = jnp.stack(tap_sums)
    spill = passed_along(d_extended[:, : tap_count - 1, :], "seq", -1)
    d_keys = (
        d_extended[:, tap_count - 1 :, :]
        + jnp.pad(spill, ((0, 0), (block_len - tap_count + 1, 0), (0, 0)))
    ).astype(jnp.bfloat16)
    grad_query = jnp.einsum("btd,btc->dc", normed, d_queries, preferred_element_type=jnp.float32)
    grad_key = jnp.einsum("btd,btc->dc", normed, d_keys, preferred_element_type=jnp.float32)
    grad_value = jnp.einsum("btd,btc->dc", normed, d_values, preferred_element_type=jnp.float32)
    d_first_part = jnp.einsum(
        "btc,dc->btd", d_queries, query_weight, preferred_element_type=jnp.float32
    )
    d_first_part = d_first_part + jnp.einsum(
        "btc,dc->btd", d_keys, key_weight, preferred_element_type=jnp.float32
    )
    d_first_part = d_first_part + jnp.einsum(
        "btc,dc->btd", d_values, value_weight, preferred_element_type=jnp.float32
    )
    d_first = lax.psum(d_first_part, "tp")
    first_value, first_pull = jax.vjp(layer_norm, source, first_gain)
    d_input_norm, grad_first = first_pull(d_first)
    grad_inputs = d_residual + d_input_norm
    (
        grad_first,
        grad_query,
        grad_key,
        grad_value,
        grad_taps,
        grad_coef,
        grad_rate,
        grad_skip,
        grad_project,
        grad_second,
        grad_up,
        grad_down,
    ) = lax.psum(
        (
            grad_first,
            grad_query,
            grad_key,
            grad_value,
            grad_taps,
            grad_coef,
            grad_rate,
            grad_skip,
            grad_project,
            grad_second,
            grad_up,
            grad_down,
        ),
        "seq",
    )
    return (
        block_out,
        grad_inputs,
        grad_first,
        grad_query,
        grad_key,
        grad_value,
        grad_taps,
        grad_coef,
        grad_rate,
        grad_skip,
        grad_project,
        grad_second,
        grad_up,
        grad_down,
    )


def solution(mesh):
    return jax.shard_map(
        local,
        mesh=mesh,
        in_specs=(
            P(None, "seq", None),
            P(),
            P(),
            P(None, "tp"),
            P(None, "tp"),
            P(None, "tp"),
            P(None, "tp"),
            P("tp", None),
            P("tp", None),
            P("tp"),
            P("tp", None),
            P(),
            P(None, "tp"),
            P("tp", None),
            P(None, "seq", None),
        ),
        out_specs=(
            P(None, "seq", None),
            P(None, "seq", None),
            P(),
            P(None, "tp"),
            P(None, "tp"),
            P(None, "tp"),
            P(None, "tp"),
            P("tp", None),
            P("tp", None),
            P("tp"),
            P("tp", None),
            P(),
            P(None, "tp"),
            P("tp", None),
        ),
        check_vma=False,
    )
```

profile of v0, /device:TPU:0, one launch (start us, length us, event | category | flops | bytes accessed | tf_op | source)
XLA Modules:
  0.0 2281.5 jit_solution(13198516228330018810)
XLA Ops:
  23.4 9.7 fusion.355
  35.1 7.1 all-to-all-start
  42.4 46.5 %all-to-all-done = f32[16,1,128,192]{3,0,1,2:T(8,128)S(1)} async-done(((f32[16,1,128,192]{3,0,1,2:T(8,128)}), f32[16,1,128,192]{3,0,1,2:T(8,128)S(1)}, u32[]{:S(2)}, u32[]{:S(2)}) %all-to-all-start) | async-done | bytes 1572896 | tf_op jit(solution)/shard_map/all_to_all | solution.py:49
  100.1 8.3 copy.229
  114.4 14.0 multiply_reduce_fusion.7
  128.5 167.1 %all-to-all-done.1 = f32[2,16,16,16,192]{4,3,1,0,2:T(8,128)} async-done(((f32[2,16,16,16,192]{4,3,1,0,2:T(8,128)}), f32[2,16,16,16,192]{4,3,1,0,2:T(8,128)}, u32[]{:S(2)}, u32[]{:S(2)}) %all-to-all-start.1) | async-done | bytes 6291488 | tf_op jit(solution)/shard_map/all_to_all | solution.py:64
  301.7 6.8 fusion.137
  308.6 7.2 fusion.135
  315.8 6.8 convolution_add_fusion.4
  322.6 7.0 convolution_subtract_fusion.4
  347.2 12.7 copy.239
  359.9 186.8 %all_to_all.129 = f32[2,16,2,128,192]{4,2,1,0,3:T(2,128)S(1)} all-to-all(f32[2,16,2,128,192]{4,2,1,0,3:T(2,128)} %copy.239), channel_id=1, replica_groups=mesh['seq'=8,'tp'=4] {'seq'}, dimensions={3} | all-to-all | bytes 12582912 | tf_op jit(solution)/shard_map/all_to_all | solution.py:97
  586.6 51.4 %all_to_all.130 = f32[16,8,16,192]{3,2,0,1:T(8,128)S(1)} all-to-all(f32[16,8,16,192]{3,2,0,1:T(8,128)S(1)} %copy.243), channel_id=1, replica_groups=mesh['seq'=8,'tp'=4] {'seq'}, dimensions={1} | all-to-all | bytes 3145728 | tf_op jit(solution)/shard_map/all_to_all | solution.py:105
  652.8 117.9 %all-reduce.14.cloned.1.call-done = f32[16,128,768]{2,1,0:T(8,128)} async-done(((f32[16,128,768]{2,1,0:T(8,128)}), f32[16,128,768]{2,1,0:T(8,128)}) %all-reduce.14.cloned.1.call-update) | async-done | bytes 6291472 | tf_op jit(solution)/shard_map/psum | solution.py:170
  779.6 6.1 fusion.26
  799.4 112.5 %all-reduce.16.cloned.1.call-done = f32[16,128,768]{2,1,0:T(8,128)} async-done(((f32[16,128,768]{2,1,0:T(8,128)}), f32[16,128,768]{2,1,0:T(8,128)}) %all-reduce.16.cloned.1.call-update) | async-done | bytes 6291472 | tf_op jit(solution)/shard_map/psum | solution.py:184
  911.9 6.4 multiply_reduce_fusion.8
  940.5 6.4 fusion.52
  946.9 6.4 fusion.54
  953.3 35.3 %all-to-all-done.4 = f32[16,1,128,192]{3,0,1,2:T(8,128)} async-done(((f32[16,1,128,192]{3,0,1,2:T(8,128)}), f32[16,1,128,192]{3,0,1,2:T(8,128)}, u32[]{:S(2)}, u32[]{:S(2)}) %all-to-all-start.4) | async-done | bytes 1572896 | tf_op jit(solution)/shard_map/all_to_all | solution.py:49
  988.6 6.2 fusion.56
  994.8 10.9 add_bitcast_fusion
  1007.3 8.2 copy.250
  1024.9 8.2 copy.269
  1033.1 169.4 %all-to-all-done.5 = f32[2,16,16,16,192]{4,3,1,0,2:T(8,128)} async-done(((f32[2,16,16,16,192]{4,3,1,0,2:T(8,128)}), f32[2,16,16,16,192]{4,3,1,0,2:T(8,128)}, u32[]{:S(2)}, u32[]{:S(2)}) %all-to-all-start.5) | async-done | bytes 6291488 | tf_op jit(solution)/shard_map/all_to_all | solution.py:64
  1214.0 6.8 fusion.131
  1220.8 7.0 fusion.129
  1227.8 6.8 convolution_add_fusion.2
  1234.7 7.0 convolution_subtract_fusion.2
  1259.4 12.7 copy.256
  1272.1 117.5 %all-to-all-done.9 = f32[2,16,16,16,192]{4,3,1,0,2:T(8,128)} async-done(((f32[2,16,16,16,192]{4,3,1,0,2:T(8,128)}), f32[2,16,16,16,192]{4,3,1,0,2:T(8,128)}, u32[]{:S(2)}, u32[]{:S(2)}) %all-to-all-start.9) | async-done | bytes 6291488 | tf_op jit(solution)/shard_map/all_to_all | solution.py:64
  1394.7 8.2 convolution_bitcast_fusion
  1421.4 8.1 copy.334
  1429.5 147.4 %all-to-all-done.6 = f32[2,16,2,128,192]{4,2,1,0,3:T(2,128)} async-done(((f32[2,16,2,128,192]{4,2,1,0,3:T(2,128)}), f32[2,16,2,128,192]{4,2,1,0,3:T(2,128)}, u32[]{:S(2)}, u32[]{:S(2)}) %all-to-all-start.6) | async-done | bytes 6291488 | tf_op jit(solution)/shard_map/all_to_all | solution.py:97
  1576.9 8.6 copy.257
  1609.6 6.1 squeeze.43
  1630.8 7.0 fusion.125
  1637.8 7.0 fusion.123
  1644.8 6.9 convolution_add_fusion
  1651.8 8.3 fusion.35
  1661.4 12.7 all-to-all-done.7
  1680.2 8.6 multiply_reduce_fusion.14
  1703.7 8.2 add_add_fusion.3
  1713.3 35.0 %fusion.30 = (f32[192,64]{1,0:T(8,128)S(1)}, f32[192,64]{1,0:T(8,128)S(1)}, f32[192,64]{1,0:T(8,128)S(1)}, f32[192,64]{1,0:T(8,128)S(1)}, f32[192,64]{1,0:T(8,12...) fusion(f32[192,64]{1,0:T(8,128)S(1)} %copy-done.44, f32[192,64]{1,0:T(8,128)S(1)} %copy-done.48, ...), kind=kLoop, calls=%fused_computation.71 | loop fusion | flops 144605184 | bytes 1133568 | tf_op jit(solution)/shard_map/transpose(jvp())/reduce_sum | solution.py:30
  1755.2 178.1 %all-reduce.22.cloned.1.call-done = (f32[16,128,768]{2,1,0:T(8,128)}, f32[16,128,768]{2,1,0:T(8,128)}) async-done(((f32[16,128,768]{2,1,0:T(8,128)}, f32[16,128,768]{2,1,0:T(8,128)}), (f32[16,128,768]{2,1,0:T(8,128)}, f32[16,128,768]{2,1,0:T(8,128)})) %all-reduce.22.cloned.1.call-update) | async-done | bytes 12582928 | tf_op jit(solution)/shard_map/psum | solution.py:175
  1948.5 15.6 add_add_fusion.2
  1964.1 51.2 %all-reduce.18.cloned.1.call-done = (f32[768]{0:T(1024)}, f32[4,192]{1,0:T(4,128)}, f32[192,64]{1,0:T(8,128)}, f32[192,64]{1,0:T(8,128)}, f32[192]{0:T(256)}, /*index=5*/f32[768]{0:T(1024)}) async-done(((f32[768]{0:T(1024)}, f32[4,192]{1,0:T(4,128)}, f32[192,64]{1,0:T(8,128)}, f32[192,64]{1,0:T(8,128)}, f32[192]{0:T(256)}, /*index=5*/f32[768]{0:T(1024)}), (f32[768]{0:T(1024)}, f32[4,192]{1,0:T(4,128)}, ...) | async-done | bytes 108304 | tf_op jit(solution)/shard_map/psum | solution.py:262
  2018.5 241.1 %all-reduce.20.cloned.1.call-done = (f32[768,192]{0,1:T(8,128)}, f32[768,192]{0,1:T(8,128)}, f32[768,192]{0,1:T(8,128)}, f32[192,768]{1,0:T(8,128)}, f32[768,768]{1,0:T(8,128)}, /*index=5*/f32[768,768]{1,0:T(8,128)}) async-done(((f32[768,192]{0,1:T(8,128)}, f32[768,192]{0,1:T(8,128)}, f32[768,192]{0,1:T(8,128)}, f32[192,768]{1,0:T(8,128)}, f32[768,768]{1,0:T(8,128)}, /*index=5*/f32[768,768]{1,0:T(8,128)}), ...) | async-done | bytes 7077904 | tf_op jit(solution)/shard_map/psum | solution.py:262
  (344 shorter events, 324.7 us)
Async XLA Ops:
  7.2 768.8 %copy-start = (bf16[768,768]{1,0:T(8,128)(2,1)S(1)}, bf16[768,768]{1,0:T(8,128)(2,1)}, u32[]{:S(2)}) copy-start(bf16[768,768]{1,0:T(8,128)(2,1)} %param.27) | copy-start | bytes 3538948
  10.1 632.1 %copy-start.63 = (f32[16,128]{1,0:T(8,128)}, f32[16,128]{1,0:T(8,128)S(1)}, u32[]{:S(2)}) copy-start(f32[16,128]{1,0:T(8,128)S(1)} %broadcast_multiply_fusion.7) | copy-start | bytes 24580
  11.3 631.0 %copy-start.69 = (f32[16,128]{1,0:T(8,128)}, f32[16,128]{1,0:T(8,128)S(1)}, u32[]{:S(2)}) copy-start(f32[16,128]{1,0:T(8,128)S(1)} %fusion.170) | copy-start | bytes 24580
  14.0 9.4 copy-start.59
  15.1 6.6 collective-permute-start
  20.0 13.1 copy-start.87
  20.0 13.1 copy-start.89
  20.0 13.1 copy-start.91
  20.1 13.1 copy-start.93
  35.1 53.7 %all-to-all-start = ((f32[16,1,128,192]{3,0,1,2:T(8,128)}), f32[16,1,128,192]{3,0,1,2:T(8,128)S(1)}, u32[]{:S(2)}, u32[]{:S(2)}) async-start(f32[16,1,128,192]{3,0,1,2:T(8,128)} %copy.225), calls=%async_computation | async-start | bytes 4194304 | tf_op jit(solution)/shard_map/all_to_all | solution.py:49
  108.4 187.1 %all-to-all-start.1 = ((f32[2,16,16,16,192]{4,3,1,0,2:T(8,128)}), f32[2,16,16,16,192]{4,3,1,0,2:T(8,128)}, u32[]{:S(2)}, u32[]{:S(2)}) async-start(f32[2,16,16,16,192]{4,3,1,0,2:T(8,128)} %copy.229), calls=%async_computation.1 | async-start | bytes 16777216 | tf_op jit(solution)/shard_map/all_to_all | solution.py:64
  113.6 657.2 %all-reduce.14.cloned.1.call-start = ((), (), s32[]{:S(2)}) async-start(), calls=%async_computation.10 | async-start | bytes 12582912 | tf_op jit(solution)/shard_map/psum | solution.py:170
  113.7 14.6 copy-start.53
  113.8 14.5 copy-start.39
  113.9 14.4 copy-start.80
  114.1 225.7 %copy-start.81 = (f32[2,128]{1,0:T(2,128)}, f32[2,128]{1,0:T(2,128)S(1)}, u32[]{:S(2)}) copy-start(f32[2,128]{1,0:T(2,128)S(1)} %get-tuple-element.113) | copy-start | bytes 3076
  114.1 225.7 %copy-start.83 = (f32[2,128]{1,0:T(2,128)}, f32[2,128]{1,0:T(2,128)S(1)}, u32[]{:S(2)}) copy-start(f32[2,128]{1,0:T(2,128)S(1)} %get-tuple-element.114) | copy-start | bytes 3076
  114.2 14.1 copy-start.78
  114.2 14.1 copy-start.79
  114.3 14.1 copy-start.41
  114.3 14.1 copy-start.43
  114.3 14.1 copy-start.45
  114.3 14.1 copy-start.47
  114.3 14.1 copy-start.49
  114.3 14.1 copy-start.51
  128.5 211.3 %copy-start.18 = (f32[2,128,192]{1,2,0:T(8,128)}, f32[2,128,192]{1,2,0:T(8,128)S(1)}, u32[]{:S(2)}) copy-start(f32[2,128,192]{1,2,0:T(8,128)S(1)} %get-tuple-element.120) | copy-start | bytes 589828
  128.5 211.3 %copy-start.20 = (f32[2,128,192]{1,2,0:T(8,128)}, f32[2,128,192]{1,2,0:T(8,128)S(1)}, u32[]{:S(2)}) copy-start(f32[2,128,192]{1,2,0:T(8,128)S(1)} %get-tuple-element.121) | copy-start | bytes 589828
  652.1 259.8 %all-reduce.16.cloned.1.call-start = ((), (), s32[]{:S(2)}) async-start(), calls=%async_computation.11 | async-start | bytes 12582912 | tf_op jit(solution)/shard_map/psum | solution.py:184
  793.9 140.6 %all-to-all-start.8 = ((f32[16,1,128,192]{3,0,1,2:T(8,128)}), f32[16,1,128,192]{3,0,1,2:T(8,128)S(1)}, u32[]{:S(2)}, u32[]{:S(2)}) async-start(f32[16,1,128,192]{3,0,1,2:T(8,128)} %copy.265), calls=%async_computation.8 | async-start | bytes 4194304 | tf_op jit(solution)/shard_map/all_to_all | solution.py:49
  934.5 54.1 %all-to-all-start.4 = ((f32[16,1,128,192]{3,0,1,2:T(8,128)}), f32[16,1,128,192]{3,0,1,2:T(8,128)}, u32[]{:S(2)}, u32[]{:S(2)}) async-start(f32[16,1,128,192]{3,0,1,2:T(8,128)} %copy.246), calls=%async_computation.4 | async-start | bytes 4194304 | tf_op jit(solution)/shard_map/all_to_all | solution.py:49
  1015.5 187.0 %all-to-all-start.5 = ((f32[2,16,16,16,192]{4,3,1,0,2:T(8,128)}), f32[2,16,16,16,192]{4,3,1,0,2:T(8,128)}, u32[]{:S(2)}, u32[]{:S(2)}) async-start(f32[2,16,16,16,192]{4,3,1,0,2:T(8,128)} %copy.250), calls=%async_computation.5 | async-start | bytes 16777216 | tf_op jit(solution)/shard_map/all_to_all | solution.py:64
  1202.5 187.1 %all-to-all-start.9 = ((f32[2,16,16,16,192]{4,3,1,0,2:T(8,128)}), f32[2,16,16,16,192]{4,3,1,0,2:T(8,128)}, u32[]{:S(2)}, u32[]{:S(2)}) async-start(f32[2,16,16,16,192]{4,3,1,0,2:T(8,128)} %copy.269), calls=%async_computation.9 | async-start | bytes 16777216 | tf_op jit(solution)/shard_map/all_to_all | solution.py:64
  1234.7 17.3 copy-start.6
  1241.7 10.2 copy-start.8
  1389.6 13.3 slice-start
  1389.6 187.3 %all-to-all-start.6 = ((f32[2,16,2,128,192]{4,2,1,0,3:T(2,128)}), f32[2,16,2,128,192]{4,2,1,0,3:T(2,128)}, u32[]{:S(2)}, u32[]{:S(2)}) async-start(f32[2,16,2,128,192]{4,2,1,0,3:T(2,128)} %copy.256), calls=%async_computation.6 | async-start | bytes 16777216 | tf_op jit(solution)/shard_map/all_to_all | solution.py:97
  1621.8 52.4 %all-to-all-start.7 = ((f32[16,8,16,192]{3,2,0,1:T(8,128)}), f32[16,8,16,192]{3,2,0,1:T(8,128)}, u32[]{:S(2)}, u32[]{:S(2)}) async-start(f32[16,8,16,192]{3,2,0,1:T(8,128)} %copy.260), calls=%async_computation.7 | async-start | bytes 4194304 | tf_op jit(solution)/shard_map/all_to_all | solution.py:105
  1626.1 307.2 %all-reduce.22.cloned.1.call-start = ((), (), s32[]{:S(2)}) async-start(), calls=%async_computation.14 | async-start | bytes 25165824 | tf_op jit(solution)/shard_map/psum | solution.py:175
  1660.7 19.4 copy-start.25
  1660.7 19.4 copy-start.86
  1694.4 6.0 collective-permute-start.1
  1712.0 37.0 %copy-start.54 = (f32[192,64]{1,0:T(8,128)S(1)}, f32[192,64]{1,0:T(8,128)}, u32[]{:S(2)}) copy-start(f32[192,64]{1,0:T(8,128)} %copy-done.53) | copy-start | bytes 147460
  1712.1 303.3 %all-reduce.18.cloned.1.call-start = ((), (), s32[]{:S(2)}) async-start(), calls=%async_computation.12 | async-start | bytes 419840 | tf_op jit(solution)/shard_map/psum | solution.py:262
  1751.0 182.3 %copy-start.76 = (f32[768]{0:T(1024)S(1)}, f32[768]{0:T(1024)}, u32[]{:S(2)}) copy-start(f32[768]{0:T(1024)} %param.17) | copy-start | bytes 9220
  1943.7 316.0 %all-reduce.20.cloned.1.call-start = ((), (), s32[]{:S(2)}) async-start(), calls=%async_computation.13 | async-start | bytes 14155776 | tf_op jit(solution)/shard_map/psum | solution.py:262
  2015.3 256.1 %copy-start.96 = (f32[768]{0:T(1024)S(1)}, f32[768]{0:T(1024)}, u32[]{:S(2)}) copy-start(f32[768]{0:T(1024)} %get-tuple-element.133) | copy-start | bytes 9220
  2259.7 12.3 copy-start.35
  2263.0 10.4 copy-start.34
  (71 other events, 291.2 us)
Sparse Core Ops, SparseCore 0:
  652.2 118.4 all-reduce.13
  792.1 119.7 all-reduce.15
  1712.2 221.1 all-reduce.21
  1943.8 71.4 all-reduce.17
  2022.2 237.4 all-reduce.19
where the time goes:
time: 2290 us; the launch traced here: 2280 us
  waiting for transfers between devices  1400 us (61%)
  matrix products  252 us (11%)
  blocking collectives  238 us (10%)
  local copies, waits for them, and re-layouts  198 us (9%)
  other arithmetic  128 us (6%)
  starting transfers between devices  50.5 us (2%)
    all_to_all x3, waiting for transfers between devices, to_bins(): lax.all_to_all(jnp.stack([turned_re, turned_im]), 'seq', split_axis=2, co...  454 us
    psum x2, waiting for transfers between devices, local(): lax.psum((grad_first, grad_query, grad_key, grad_value, grad_taps, grad_c...  292 us
    all_to_all x1, blocking collectives, from_bins(): lax.all_to_all(jnp.stack([turned_re, turned_im]), 'seq', split_axis=3, co...  187 us
    psum x1, waiting for transfers between devices, local(): lowered = lax.psum(project(hidden, down_weight), 'tp')  178 us
    all_to_all x1, waiting for transfers between devices, from_bins(): lax.all_to_all(jnp.stack([turned_re, turned_im]), 'seq', split_axis=3, co...  147 us
    psum x1, waiting for transfers between devices, local(): mixer = lax.psum(project(gated_out, project_weight), 'tp')  118 us
    psum x1, waiting for transfers between devices, local(): lax.psum(jnp.einsum('btf,df->btd', d_up, up_weight, preferred_element_typ...  113 us
    all_to_all x3, waiting for transfers between devices, to_bins(): lax.all_to_all(signal.reshape(num_seqs, 1, block_len, channels), 'seq', s...  81.8 us
  transfers between devices with their start and end apart: 15, of which 14 were waited for; matrix products, arithmetic and copies ran while one was open for 11% of the time, Pallas kernels for 0%

commit v1 on v0

--- a/solution.py
+++ b/solution.py
@@ -102,7 +102,19 @@
         jnp.einsum("bqmc,qp->bpmc", parted[0], jnp.cos(outer), precision=exact_mode)
         - jnp.einsum("bqmc,qp->bpmc", parted[1], jnp.sin(outer), precision=exact_mode)
     ) / total
-    joined = lax.all_to_all(times_re, "seq", split_axis=1, concat_axis=2, tiled=True)
+    ways, here = (lax.axis_size("seq"), lax.axis_index("seq"))
+    width = times_re.shape[1] // ways
+    lengths_2 = list(times_re.shape)
+    lengths_2[1] = width
+    height = lengths_2[2]
+    lengths_2[2] = height * ways
+    full = jnp.zeros(lengths_2, times_re.dtype)
+    for mask in range(ways):
+        part = lax.dynamic_slice_in_dim(times_re, (here ^ mask) * width, width, axis=1)
+        if mask:
+            part = lax.ppermute(part, "seq", [(d, d ^ mask) for d in range(ways)])
+        full = lax.dynamic_update_slice_in_dim(full, part, (here ^ mask) * height, axis=2)
+    joined = full
     return joined.reshape(num_seqs, block_len, channels)
 
 

time: 2290 us -> 2410 us (1.052)
  blocking collectives: 238 us -> 0 us
  local copies, waits for them, and re-layouts: 198 us -> 376 us
  waiting for transfers between devices: 1400 us -> 1550 us
    all_to_all x2 -> x0, blocking collectives: 238 us -> none  [the longest x1 187 us: from_bins(): lax.all_to_all(jnp.stack([turned_re, turned_im]), 'seq', split_axis=3, co...]
    dynamic_update_slice x0 -> x16, local copies, waits for them, and re-layouts: none -> 162 us  [from_bins(): lax.dynamic_update_slice_in_dim(full, part, (here ^ mask) * height, axis=2)]
    all_to_all x1 -> x2, waiting for transfers between devices: 147 us -> 297 us  [from_bins(): lax.all_to_all(jnp.stack([turned_re, turned_im]), 'seq', split_axis=3, co...]
  transfers between devices with their start and end apart: 15 -> 29, of which waited for: 14 -> 16; matrix products, arithmetic and copies ran while one was open for 11% -> 18% of each run, Pallas kernels for 0% -> 0%
where the time goes in v1:
time: 2410 us; the launch traced here: 2400 us
  waiting for transfers between devices  1550 us (64%)
  local copies, waits for them, and re-layouts  376 us (16%)
  matrix products  256 us (11%)
  other arithmetic  127 us (5%)
  starting transfers between devices  70.1 us (3%)
    all_to_all x3, waiting for transfers between devices, to_bins(): lax.all_to_all(jnp.stack([turned_re, turned_im]), 'seq', split_axis=2, co...  454 us
    all_to_all x2, waiting for transfers between devices, from_bins(): lax.all_to_all(jnp.stack([turned_re, turned_im]), 'seq', split_axis=3, co...  297 us
    psum x2, waiting for transfers between devices, local(): lax.psum((grad_first, grad_query, grad_key, grad_value, grad_taps, grad_c...  292 us
    psum x1, waiting for transfers between devices, local(): lowered = lax.psum(project(hidden, down_weight), 'tp')  180 us
    dynamic_update_slice x16, local copies, waits for them, and re-layouts, from_bins(): lax.dynamic_update_slice_in_dim(full, part, (here ^ mask) * height, axis=2)  162 us
    psum x1, waiting for transfers between devices, local(): mixer = lax.psum(project(gated_out, project_weight), 'tp')  121 us
    psum x1, waiting for transfers between devices, local(): lax.psum(jnp.einsum('btf,df->btd', d_up, up_weight, preferred_element_typ...  113 us
    all_to_all x3, waiting for transfers between devices, to_bins(): lax.all_to_all(signal.reshape(num_seqs, 1, block_len, channels), 'seq', s...  82 us
  transfers between devices with their start and end apart: 29, of which 16 were waited for; matrix products, arithmetic and copies ran while one was open for 18% of the time, Pallas kernels for 0%

profile of v1, /device:TPU:0, one launch (start us, length us, event | category | flops | bytes accessed | tf_op | source)
XLA Modules:
  0.0 2398.8 jit_solution(7498581911325396673)
XLA Ops:
  23.4 9.6 fusion.345
  42.0 46.7 %all-to-all-done = f32[16,1,128,192]{3,0,1,2:T(8,128)S(1)} async-done(((f32[16,1,128,192]{3,0,1,2:T(8,128)}), f32[16,1,128,192]{3,0,1,2:T(8,128)S(1)}, u32[]{:S(2)}, u32[]{:S(2)}) %all-to-all-start) | async-done | bytes 1572896 | tf_op jit(solution)/shard_map/all_to_all | solution.py:49
  100.0 8.6 copy.275
  114.5 14.0 multiply_reduce_fusion.7
  128.6 167.2 %all-to-all-done.1 = f32[2,16,16,16,192]{4,3,1,0,2:T(8,128)} async-done(((f32[2,16,16,16,192]{4,3,1,0,2:T(8,128)}), f32[2,16,16,16,192]{4,3,1,0,2:T(8,128)}, u32[]{:S(2)}, u32[]{:S(2)}) %all-to-all-start.1) | async-done | bytes 6291488 | tf_op jit(solution)/shard_map/all_to_all | solution.py:64
  322.6 7.2 convolution_subtract_fusion.4
  347.2 12.7 copy.285
  365.0 181.8 %all-to-all-done.2 = f32[2,16,2,128,192]{4,2,1,0,3:T(2,128)} async-done(((f32[2,16,2,128,192]{4,2,1,0,3:T(2,128)}), f32[2,16,2,128,192]{4,2,1,0,3:T(2,128)}, u32[]{:S(2)}, u32[]{:S(2)}) %all-to-all-start.2) | async-done | bytes 6291488 | tf_op jit(solution)/shard_map/all_to_all | solution.py:97
  546.8 8.2 copy.286
  614.5 7.6 dynamic_update_slice.64
  622.6 10.7 dynamic_update_slice.65
  634.7 10.9 dynamic_update_slice.66
  647.1 10.7 dynamic_update_slice.67
  659.2 10.7 dynamic_update_slice.68
  670.4 10.7 dynamic_update_slice.69
  682.8 9.9 dynamic_update_slice.70
  695.3 9.7 dynamic_update_slice.71
  715.7 120.5 %all-reduce.14.cloned.1.call-done = f32[16,128,768]{2,1,0:T(8,128)} async-done(((f32[16,128,768]{2,1,0:T(8,128)}), f32[16,128,768]{2,1,0:T(8,128)}) %all-reduce.14.cloned.1.call-update) | async-done | bytes 6291472 | tf_op jit(solution)/shard_map/psum | solution.py:182
  865.1 112.5 %all-reduce.16.cloned.1.call-done = f32[16,128,768]{2,1,0:T(8,128)} async-done(((f32[16,128,768]{2,1,0:T(8,128)}), f32[16,128,768]{2,1,0:T(8,128)}) %all-reduce.16.cloned.1.call-update) | async-done | bytes 6291472 | tf_op jit(solution)/shard_map/psum | solution.py:196
  1018.9 35.3 %all-to-all-done.3 = f32[16,1,128,192]{3,0,1,2:T(8,128)} async-done(((f32[16,1,128,192]{3,0,1,2:T(8,128)}), f32[16,1,128,192]{3,0,1,2:T(8,128)}, u32[]{:S(2)}, u32[]{:S(2)}) %all-to-all-start.3) | async-done | bytes 1572896 | tf_op jit(solution)/shard_map/all_to_all | solution.py:49
  1060.4 10.9 add_bitcast_fusion
  1072.9 8.2 copy.301
  1090.5 8.2 copy.325
  1098.7 169.4 %all-to-all-done.4 = f32[2,16,16,16,192]{4,3,1,0,2:T(8,128)} async-done(((f32[2,16,16,16,192]{4,3,1,0,2:T(8,128)}), f32[2,16,16,16,192]{4,3,1,0,2:T(8,128)}, u32[]{:S(2)}, u32[]{:S(2)}) %all-to-all-start.4) | async-done | bytes 6291488 | tf_op jit(solution)/shard_map/all_to_all | solution.py:64
  1300.3 7.2 convolution_subtract_fusion.2
  1324.8 12.7 copy.307
  1337.5 117.6 %all-to-all-done.7 = f32[2,16,16,16,192]{4,3,1,0,2:T(8,128)} async-done(((f32[2,16,16,16,192]{4,3,1,0,2:T(8,128)}), f32[2,16,16,16,192]{4,3,1,0,2:T(8,128)}, u32[]{:S(2)}, u32[]{:S(2)}) %all-to-all-start.7) | async-done | bytes 6291488 | tf_op jit(solution)/shard_map/all_to_all | solution.py:64
  1460.2 8.2 convolution_bitcast_fusion
  1468.4 9.4 fusion.71
  1504.0 7.0 fusion.123
  1517.9 8.9 fusion.35
  1526.9 115.6 %all-to-all-done.5 = f32[2,16,2,128,192]{4,2,1,0,3:T(2,128)} async-done(((f32[2,16,2,128,192]{4,2,1,0,3:T(2,128)}), f32[2,16,2,128,192]{4,2,1,0,3:T(2,128)}, u32[]{:S(2)}, u32[]{:S(2)}) %all-to-all-start.5) | async-done | bytes 6291488 | tf_op jit(solution)/shard_map/all_to_all | solution.py:97
  1642.5 8.2 copy.308
  1709.2 7.6 dynamic_update_slice.72
  1717.3 10.7 dynamic_update_slice.73
  1728.5 10.9 dynamic_update_slice.74
  1739.9 10.7 dynamic_update_slice.75
  1751.1 10.7 dynamic_update_slice.76
  1762.3 10.7 dynamic_update_slice.77
  1774.7 9.9 dynamic_update_slice.78
  1786.2 9.7 dynamic_update_slice.79
  1796.0 8.0 multiply_reduce_fusion.14
  1819.1 8.2 add_add_fusion.3
  1828.6 35.0 %fusion.30 = (f32[192,64]{1,0:T(8,128)S(1)}, f32[192,64]{1,0:T(8,128)S(1)}, f32[192,64]{1,0:T(8,128)S(1)}, f32[192,64]{1,0:T(8,128)S(1)}, f32[192,64]{1,0:T(8,12...) fusion(f32[192,64]{1,0:T(8,128)S(1)} %copy-done.44, f32[192,64]{1,0:T(8,128)S(1)} %copy-done.48, ...), kind=kLoop, calls=%fused_computation.71 | loop fusion | flops 144605184 | bytes 1133568 | tf_op jit(solution)/shard_map/transpose(jvp())/reduce_sum | solution.py:30
  1870.5 179.9 %all-reduce.22.cloned.1.call-done = (f32[16,128,768]{2,1,0:T(8,128)}, f32[16,128,768]{2,1,0:T(8,128)}) async-done(((f32[16,128,768]{2,1,0:T(8,128)}, f32[16,128,768]{2,1,0:T(8,128)}), (f32[16,128,768]{2,1,0:T(8,128)}, f32[16,128,768]{2,1,0:T(8,128)})) %all-reduce.22.cloned.1.call-update) | async-done | bytes 12582928 | tf_op jit(solution)/shard_map/psum | solution.py:187
  2065.5 15.6 add_add_fusion.2
  2081.1 51.3 %all-reduce.18.cloned.1.call-done = (f32[768]{0:T(1024)}, f32[4,192]{1,0:T(4,128)}, f32[192,64]{1,0:T(8,128)}, f32[192,64]{1,0:T(8,128)}, f32[192]{0:T(256)}, /*index=5*/f32[768]{0:T(1024)}) async-done(((f32[768]{0:T(1024)}, f32[4,192]{1,0:T(4,128)}, f32[192,64]{1,0:T(8,128)}, f32[192,64]{1,0:T(8,128)}, f32[192]{0:T(256)}, /*index=5*/f32[768]{0:T(1024)}), (f32[768]{0:T(1024)}, f32[4,192]{1,0:T(4,128)}, ...) | async-done | bytes 108304 | tf_op jit(solution)/shard_map/psum | solution.py:274
  2135.6 241.1 %all-reduce.20.cloned.1.call-done = (f32[768,192]{0,1:T(8,128)}, f32[768,192]{0,1:T(8,128)}, f32[768,192]{0,1:T(8,128)}, f32[192,768]{1,0:T(8,128)}, f32[768,768]{1,0:T(8,128)}, /*index=5*/f32[768,768]{1,0:T(8,128)}) async-done(((f32[768,192]{0,1:T(8,128)}, f32[768,192]{0,1:T(8,128)}, f32[768,192]{0,1:T(8,128)}, f32[192,768]{1,0:T(8,128)}, f32[768,768]{1,0:T(8,128)}, /*index=5*/f32[768,768]{1,0:T(8,128)}), ...) | async-done | bytes 7077904 | tf_op jit(solution)/shard_map/psum | solution.py:274
  (440 shorter events, 466.0 us)
Async XLA Ops:
  7.2 834.3 %copy-start = (bf16[768,768]{1,0:T(8,128)(2,1)S(1)}, bf16[768,768]{1,0:T(8,128)(2,1)}, u32[]{:S(2)}) copy-start(bf16[768,768]{1,0:T(8,128)(2,1)} %param.27) | copy-start | bytes 3538948
  10.1 694.9 %copy-start.71 = (f32[16,128]{1,0:T(8,128)}, f32[16,128]{1,0:T(8,128)S(1)}, u32[]{:S(2)}) copy-start(f32[16,128]{1,0:T(8,128)S(1)} %broadcast_multiply_fusion.7) | copy-start | bytes 24580
  11.3 693.8 %copy-start.81 = (f32[16,128]{1,0:T(8,128)}, f32[16,128]{1,0:T(8,128)S(1)}, u32[]{:S(2)}) copy-start(f32[16,128]{1,0:T(8,128)S(1)} %fusion.170) | copy-start | bytes 24580
  15.1 6.6 collective-permute-start
  35.0 53.8 %all-to-all-start = ((f32[16,1,128,192]{3,0,1,2:T(8,128)}), f32[16,1,128,192]{3,0,1,2:T(8,128)S(1)}, u32[]{:S(2)}, u32[]{:S(2)}) async-start(f32[16,1,128,192]{3,0,1,2:T(8,128)} %copy.271), calls=%async_computation | async-start | bytes 4194304 | tf_op jit(solution)/shard_map/all_to_all | solution.py:49
  42.0 56.4 %copy-start.75 = (f32[16,16]{0,1:T(8,128)}, f32[16,16]{0,1:T(8,128)S(1)}, u32[]{:S(2)}) copy-start(f32[16,16]{0,1:T(8,128)S(1)} %get-tuple-element.131) | copy-start | bytes 3076
  42.0 56.4 %copy-start.77 = (f32[16,16]{0,1:T(8,128)}, f32[16,16]{0,1:T(8,128)S(1)}, u32[]{:S(2)}) copy-start(f32[16,16]{0,1:T(8,128)S(1)} %get-tuple-element.132) | copy-start | bytes 3076
  108.7 187.1 %all-to-all-start.1 = ((f32[2,16,16,16,192]{4,3,1,0,2:T(8,128)}), f32[2,16,16,16,192]{4,3,1,0,2:T(8,128)}, u32[]{:S(2)}, u32[]{:S(2)}) async-start(f32[2,16,16,16,192]{4,3,1,0,2:T(8,128)} %copy.275), calls=%async_computation.1 | async-start | bytes 16777216 | tf_op jit(solution)/shard_map/all_to_all | solution.py:64
  114.2 225.6 %copy-start.94 = (f32[2,128]{1,0:T(2,128)}, f32[2,128]{1,0:T(2,128)S(1)}, u32[]{:S(2)}) copy-start(f32[2,128]{1,0:T(2,128)S(1)} %get-tuple-element.129) | copy-start | bytes 3076
  114.2 225.6 %copy-start.96 = (f32[2,128]{1,0:T(2,128)}, f32[2,128]{1,0:T(2,128)S(1)}, u32[]{:S(2)}) copy-start(f32[2,128]{1,0:T(2,128)S(1)} %get-tuple-element.130) | copy-start | bytes 3076
  128.6 211.2 %copy-start.18 = (f32[2,128,192]{1,2,0:T(8,128)}, f32[2,128,192]{1,2,0:T(8,128)S(1)}, u32[]{:S(2)}) copy-start(f32[2,128,192]{1,2,0:T(8,128)S(1)} %get-tuple-element.136) | copy-start | bytes 589828
  128.6 211.2 %copy-start.20 = (f32[2,128,192]{1,2,0:T(8,128)}, f32[2,128,192]{1,2,0:T(8,128)S(1)}, u32[]{:S(2)}) copy-start(f32[2,128,192]{1,2,0:T(8,128)S(1)} %get-tuple-element.137) | copy-start | bytes 589828
  359.9 186.9 %all-to-all-start.2 = ((f32[2,16,2,128,192]{4,2,1,0,3:T(2,128)}), f32[2,16,2,128,192]{4,2,1,0,3:T(2,128)}, u32[]{:S(2)}, u32[]{:S(2)}) async-start(f32[2,16,2,128,192]{4,2,1,0,3:T(2,128)} %copy.285), calls=%async_computation.2 | async-start | bytes 16777216 | tf_op jit(solution)/shard_map/all_to_all | solution.py:97
  364.9 471.4 %all-reduce.14.cloned.1.call-start = ((), (), s32[]{:S(2)}) async-start(), calls=%async_computation.8 | async-start | bytes 12582912 | tf_op jit(solution)/shard_map/psum | solution.py:182
  591.8 10.3 collective-permute-start.1
  593.4 17.4 collective-permute-start.2
  594.2 51.4 %collective-permute-start.3 = (f32[16,1,16,192]{3,2,1,0:T(8,128)}, f32[16,1,16,192]{3,2,1,0:T(8,128)}, u32[]{:S(2)}, u32[]{:S(2)}) collective-permute-start(f32[16,1,16,192]{3,2,1,0:T(8,128)} %bitcast.446), channel_id=1, source_target_pairs={{0,12},{4,8},{8,4},{12,0},{16,28},{20,24},{24,20},{28,16},{1,13},{... | collective-permute-start | bytes 589832 | tf_op jit(solution)/shard_map/ppermute | solution.py:115
  596.9 60.8 %collective-permute-start.4 = (f32[16,1,16,192]{3,2,1,0:T(8,128)}, f32[16,1,16,192]{3,2,1,0:T(8,128)}, u32[]{:S(2)}, u32[]{:S(2)}) collective-permute-start(f32[16,1,16,192]{3,2,1,0:T(8,128)} %bitcast.445), channel_id=1, source_target_pairs={{0,16},{4,20},{8,24},{12,28},{16,0},{20,4},{24,8},{28,12},{1,17},{... | collective-permute-start | bytes 589832 | tf_op jit(solution)/shard_map/ppermute | solution.py:115
  598.9 71.1 %collective-permute-start.5 = (f32[16,1,16,192]{3,2,1,0:T(8,128)}, f32[16,1,16,192]{3,2,1,0:T(8,128)S(1)}, u32[]{:S(2)}, u32[]{:S(2)}) collective-permute-start(f32[16,1,16,192]{3,2,1,0:T(8,128)} %bitcast.444), channel_id=1, source_target_pairs={{0,20},{4,16},{8,28},{12,24},{16,4},{20,0},{24,12},{28,8},{1,21},{... | collective-permute-start | bytes 589832 | tf_op jit(solution)/shard_map/ppermute | solution.py:115
  602.2 78.9 %collective-permute-start.6 = (f32[16,1,16,192]{3,2,1,0:T(8,128)}, f32[16,1,16,192]{3,2,1,0:T(8,128)S(1)}, u32[]{:S(2)}, u32[]{:S(2)}) collective-permute-start(f32[16,1,16,192]{3,2,1,0:T(8,128)} %bitcast.443), channel_id=1, source_target_pairs={{0,24},{4,28},{8,16},{12,20},{16,8},{20,12},{24,0},{28,4},{1,25},{... | collective-permute-start | bytes 589832 | tf_op jit(solution)/shard_map/ppermute | solution.py:115
  611.5 81.2 %collective-permute-start.7 = (f32[16,1,16,192]{3,2,1,0:T(8,128)}, f32[16,1,16,192]{3,2,1,0:T(8,128)}, u32[]{:S(2)}, u32[]{:S(2)}) collective-permute-start(f32[16,1,16,192]{3,2,1,0:T(8,128)} %bitcast.442), channel_id=1, source_target_pairs={{0,28},{4,24},{8,20},{12,16},{16,12},{20,8},{24,4},{28,0},{1,29},{... | collective-permute-start | bytes 589832 | tf_op jit(solution)/shard_map/ppermute | solution.py:115
  682.8 22.3 copy-start.23
  682.8 22.3 copy-start.58
  682.8 22.3 copy-start.87
  682.8 22.3 copy-start.98
  715.0 262.6 %all-reduce.16.cloned.1.call-start = ((), (), s32[]{:S(2)}) async-start(), calls=%async_computation.9 | async-start | bytes 12582912 | tf_op jit(solution)/shard_map/psum | solution.py:196
  859.6 140.6 %all-to-all-start.6 = ((f32[16,1,128,192]{3,0,1,2:T(8,128)}), f32[16,1,128,192]{3,0,1,2:T(8,128)S(1)}, u32[]{:S(2)}, u32[]{:S(2)}) async-start(f32[16,1,128,192]{3,0,1,2:T(8,128)} %copy.321), calls=%async_computation.6 | async-start | bytes 4194304 | tf_op jit(solution)/shard_map/all_to_all | solution.py:49
  1000.2 54.0 %all-to-all-start.3 = ((f32[16,1,128,192]{3,0,1,2:T(8,128)}), f32[16,1,128,192]{3,0,1,2:T(8,128)}, u32[]{:S(2)}, u32[]{:S(2)}) async-start(f32[16,1,128,192]{3,0,1,2:T(8,128)} %copy.297), calls=%async_computation.3 | async-start | bytes 4194304 | tf_op jit(solution)/shard_map/all_to_all | solution.py:49
  1018.9 41.4 %copy-start.76 = (f32[16,16]{0,1:T(8,128)S(1)}, f32[16,16]{0,1:T(8,128)}, u32[]{:S(2)}) copy-start(f32[16,16]{0,1:T(8,128)} %copy-done.75) | copy-start | bytes 3076
  1018.9 41.5 %copy-start.78 = (f32[16,16]{0,1:T(8,128)S(1)}, f32[16,16]{0,1:T(8,128)}, u32[]{:S(2)}) copy-start(f32[16,16]{0,1:T(8,128)} %copy-done.77) | copy-start | bytes 3076
  1081.1 187.0 %all-to-all-start.4 = ((f32[2,16,16,16,192]{4,3,1,0,2:T(8,128)}), f32[2,16,16,16,192]{4,3,1,0,2:T(8,128)}, u32[]{:S(2)}, u32[]{:S(2)}) async-start(f32[2,16,16,16,192]{4,3,1,0,2:T(8,128)} %copy.301), calls=%async_computation.4 | async-start | bytes 16777216 | tf_op jit(solution)/shard_map/all_to_all | solution.py:64
  1268.1 187.1 %all-to-all-start.7 = ((f32[2,16,16,16,192]{4,3,1,0,2:T(8,128)}), f32[2,16,16,16,192]{4,3,1,0,2:T(8,128)}, u32[]{:S(2)}, u32[]{:S(2)}) async-start(f32[2,16,16,16,192]{4,3,1,0,2:T(8,128)} %copy.325), calls=%async_computation.7 | async-start | bytes 16777216 | tf_op jit(solution)/shard_map/all_to_all | solution.py:64
  1455.2 187.3 %all-to-all-start.5 = ((f32[2,16,2,128,192]{4,2,1,0,3:T(2,128)}), f32[2,16,2,128,192]{4,2,1,0,3:T(2,128)}, u32[]{:S(2)}, u32[]{:S(2)}) async-start(f32[2,16,2,128,192]{4,2,1,0,3:T(2,128)} %copy.307), calls=%async_computation.5 | async-start | bytes 16777216 | tf_op jit(solution)/shard_map/all_to_all | solution.py:97
  1460.1 590.2 %all-reduce.22.cloned.1.call-start = ((), (), s32[]{:S(2)}) async-start(), calls=%async_computation.12 | async-start | bytes 25165824 | tf_op jit(solution)/shard_map/psum | solution.py:187
  1687.1 11.8 collective-permute-start.8
  1688.7 16.7 collective-permute-start.9
  1690.2 49.2 %collective-permute-start.10 = (f32[16,1,16,192]{3,2,1,0:T(8,128)}, f32[16,1,16,192]{3,2,1,0:T(8,128)S(1)}, u32[]{:S(2)}, u32[]{:S(2)}) collective-permute-start(f32[16,1,16,192]{3,2,1,0:T(8,128)} %bitcast.439), channel_id=1, source_target_pairs={{0,12},{4,8},{8,4},{12,0},{16,28},{20,24},{24,20},{28,16},{1,13},{... | collective-permute-start | bytes 589832 | tf_op jit(solution)/shard_map/ppermute | solution.py:115
  1692.9 57.7 %collective-permute-start.11 = (f32[16,1,16,192]{3,2,1,0:T(8,128)}, f32[16,1,16,192]{3,2,1,0:T(8,128)S(1)}, u32[]{:S(2)}, u32[]{:S(2)}) collective-permute-start(f32[16,1,16,192]{3,2,1,0:T(8,128)} %bitcast.438), channel_id=1, source_target_pairs={{0,16},{4,20},{8,24},{12,28},{16,0},{20,4},{24,8},{28,12},{1,17},{... | collective-permute-start | bytes 589832 | tf_op jit(solution)/shard_map/ppermute | solution.py:115
  1694.9 67.0 %collective-permute-start.12 = (f32[16,1,16,192]{3,2,1,0:T(8,128)}, f32[16,1,16,192]{3,2,1,0:T(8,128)S(1)}, u32[]{:S(2)}, u32[]{:S(2)}) collective-permute-start(f32[16,1,16,192]{3,2,1,0:T(8,128)} %bitcast.437), channel_id=1, source_target_pairs={{0,20},{4,16},{8,28},{12,24},{16,4},{20,0},{24,12},{28,8},{1,21},{... | collective-permute-start | bytes 589832 | tf_op jit(solution)/shard_map/ppermute | solution.py:115
  1698.9 74.1 %collective-permute-start.13 = (f32[16,1,16,192]{3,2,1,0:T(8,128)}, f32[16,1,16,192]{3,2,1,0:T(8,128)S(1)}, u32[]{:S(2)}, u32[]{:S(2)}) collective-permute-start(f32[16,1,16,192]{3,2,1,0:T(8,128)} %bitcast.436), channel_id=1, source_target_pairs={{0,24},{4,28},{8,16},{12,20},{16,8},{20,12},{24,0},{28,4},{1,25},{... | collective-permute-start | bytes 589832 | tf_op jit(solution)/shard_map/ppermute | solution.py:115
  1705.4 79.2 %collective-permute-start.14 = (f32[16,1,16,192]{3,2,1,0:T(8,128)}, f32[16,1,16,192]{3,2,1,0:T(8,128)S(1)}, u32[]{:S(2)}, u32[]{:S(2)}) collective-permute-start(f32[16,1,16,192]{3,2,1,0:T(8,128)} %bitcast.435), channel_id=1, source_target_pairs={{0,28},{4,24},{8,20},{12,16},{16,12},{20,8},{24,4},{28,0},{1,29},{... | collective-permute-start | bytes 589832 | tf_op jit(solution)/shard_map/ppermute | solution.py:115
  1774.7 21.3 copy-start.99
  1809.8 6.0 collective-permute-start.15
  1827.4 37.0 %copy-start.54 = (f32[192,64]{1,0:T(8,128)S(1)}, f32[192,64]{1,0:T(8,128)}, u32[]{:S(2)}) copy-start(f32[192,64]{1,0:T(8,128)} %copy-done.53) | copy-start | bytes 147460
  1827.4 305.0 %all-reduce.18.cloned.1.call-start = ((), (), s32[]{:S(2)}) async-start(), calls=%async_computation.10 | async-start | bytes 419840 | tf_op jit(solution)/shard_map/psum | solution.py:274
  1866.4 183.9 %copy-start.89 = (f32[768]{0:T(1024)S(1)}, f32[768]{0:T(1024)}, u32[]{:S(2)}) copy-start(f32[768]{0:T(1024)} %param.17) | copy-start | bytes 9220
  2060.7 316.0 %all-reduce.20.cloned.1.call-start = ((), (), s32[]{:S(2)}) async-start(), calls=%async_computation.11 | async-start | bytes 14155776 | tf_op jit(solution)/shard_map/psum | solution.py:274
  2132.4 256.1 %copy-start.109 = (f32[768]{0:T(1024)S(1)}, f32[768]{0:T(1024)}, u32[]{:S(2)}) copy-start(f32[768]{0:T(1024)} %get-tuple-element.149) | copy-start | bytes 9220
  (98 other events, 641.2 us)
Sparse Core Ops, SparseCore 0:
  715.1 121.0 all-reduce.13
  857.8 119.7 all-reduce.15
  1827.5 222.7 all-reduce.21
  2060.9 71.4 all-reduce.17
  2139.2 237.4 all-reduce.19
